TPU v7x, 32 devices: a whole 2x2x4 slice. The times are simulated.
32 devices in a mesh: gx: 4 (over z), gy: 4 (over y, core), gz: 2 (over x).
Axes of the slice: x: 2, y: 2, z: 4, core: 2. Of those that a mesh axis runs over, the one named last changes fastest.
Arguments:
- velocities: float32 [3, 1310720], P(None, ('gx', 'gy', 'gz')), may hold values from -6 to 6
- particle_cells: int32 [2, 1310720], P(None, ('gx', 'gy', 'gz')), may hold values from 0 to 4095
- grid_shift: int32 [2, 3], replicated, may hold values from -1 to 1, as said below
- axis_index: int32 [2, 16, 32, 256], P(None, 'gx', 'gy', 'gz'), may hold values from 0 to 7
- migrate_dir: int32 [1310720], P(('gx', 'gy', 'gz')), may hold values from 0 to 6, as said below
- migrate_slot: int32 [1310720], P(('gx', 'gy', 'gz')), may hold values from 0 to 159, as said below
- contact_colloid: int32 [65536], P(('gx', 'gy', 'gz')), may hold values from 0 to 8191, as said below
- contact_particle: int32 [65536], P(('gx', 'gy', 'gz')), may hold values from 0 to 40959
- contact_weight: float32 [65536], P(('gx', 'gy', 'gz')), may hold values from 0.05 to 1
- colloid_velocity: float32 [3, 8192], P(None, ('gx', 'gy', 'gz')), may hold values from -6 to 6
Outputs:
- cell_velocity: float32 [3, 16, 32, 256], P(None, 'gx', 'gy', 'gz')
- migrated: float32 [3, 1341440], P(None, ('gx', 'gy', 'gz'))
- colloid_force: float32 [3, 8192], P(None, ('gx', 'gy', 'gz'))
Inputs may be any that keep to these rules, and one draw needn't show every extreme that they name: `grid_shift`: every entry is -1 or 1, and along every dimension the sign changes from each step to the next. `migrate_dir`: code 0 keeps a particle on its device. On every device at most 160 particles take any one nonzero code, and on every device some nonzero code is taken by exactly 160 particles. `migrate_slot`: among the particles of one device with the same nonzero code, the slots are distinct and run from 0 to that code's count minus 1; the slot is 0 where the code is 0. `contact_colloid`: the owner of every contact's colloid is the contact's own device or one of its six face neighbours along gx, gy, gz (periodic).
All inputs are finite; a program needn't handle non-finite values.
Results may differ from a plain program's by a relative error of at most 0.00015.
Values sent between devices are 32-bit elements; how exact they have to be, the bound alone decides.
A program may use at most 128 MiB of HBM per device.

v0:
```python
import functools
import math

import jax
import jax.numpy as jnp
from jax import lax
from jax.experimental import pallas as pl
from jax.experimental.pallas import tpu as pltpu
from jax.sharding import PartitionSpec as P

CAP = 160
ANGLE = 130.0 * math.pi / 180.0
COS, SIN = math.cos(ANGLE), math.sin(ANGLE)
TILE = 4096
NT = (((1,), (1,)), ((), ()))
BF = jnp.bfloat16
F32 = jnp.float32


def split_index(c, low):
    if low & (low - 1) == 0:
        return c >> (low.bit_length() - 1), c & (low - 1)
    return c // low, c % low


def one_hot(row, count):
    kind = BF if count <= 256 else F32
    wide = lax.broadcasted_iota(jnp.int32, (count, row.shape[1]), 0).astype(F32).astype(kind)
    return jnp.where(wide == row.astype(F32).astype(kind), jnp.ones((), kind), jnp.zeros((), kind)).astype(BF)


def halves(x):
    high = x.astype(BF)
    return high, (x - high.astype(F32)).astype(BF)


def spread(rows, mask):
    return jnp.concatenate([mask * row for row in rows], axis=0)


def hist_tile(c, v, nhi, nlo):
    hi, lo = split_index(c, nlo)
    mask = one_hot(hi, nhi)
    rows = []
    for k in range(3):
        rows.extend(halves(v[k]))
    left = jnp.concatenate([spread(rows, mask), mask], axis=0)
    return lax.dot_general(left, one_hot(lo, nlo), NT, preferred_element_type=F32)


def mean_of(acc, mean_ref, nhi):
    count = jnp.maximum(acc[6 * nhi : 7 * nhi], 1.0)
    for k in range(3):
        total = acc[2 * k * nhi : (2 * k + 1) * nhi] + acc[(2 * k + 1) * nhi : (2 * k + 2) * nhi]
        mean_ref[k] = total / count


def signs_of(index):
    return [jnp.where((index & (1 << i)) != 0, 1.0, -1.0) for i in range(3)]


def rotate(e, v):
    along = ((1.0 - COS) / 3.0) * (e[0] * v[0] + e[1] * v[1] + e[2] * v[2])
    turn = SIN / math.sqrt(3.0)
    out = []
    for i in range(3):
        j, k = (i + 1) % 3, (i + 2) % 3
        out.append(COS * v[i] + e[i] * along + turn * (e[j] * v[k] - e[k] * v[j]))
    return out


def make_table(mean_ref, axis_ref, table_ref, nhi, nlo):
    mean = [mean_ref[k] for k in range(3)]
    index = axis_ref[...]
    turned = rotate(signs_of(index), mean)
    for k in range(3):
        high, low = halves(mean[k] - turned[k])
        table_ref[k * nhi : (k + 1) * nhi, 0:nlo] = high
        table_ref[k * nhi : (k + 1) * nhi, nlo : 2 * nlo] = low
    table_ref[3 * nhi : 4 * nhi, 0:nlo] = index.astype(F32).astype(BF)
    table_ref[3 * nhi : 4 * nhi, nlo : 2 * nlo] = jnp.zeros((nhi, nlo), BF)


def collide_tile(c, v, table, nhi, nlo):
    hi, lo = split_index(c, nlo)
    hot = one_hot(lo, nlo)
    got = jnp.dot(table, jnp.concatenate([hot, hot], axis=0), preferred_element_type=F32)
    here = lax.broadcasted_iota(jnp.int32, (nhi, c.shape[1]), 0) == hi
    picked = [
        jnp.sum(jnp.where(here, got[q * nhi : (q + 1) * nhi], 0.0), axis=0, keepdims=True)
        for q in range(4)
    ]
    turned = rotate(signs_of(picked[3].astype(jnp.int32)), v)
    return [turned[k] + picked[k] for k in range(3)]


def rows3(ref, at):
    return [ref[k : k + 1, at] for k in range(3)]


def first_kernel(
    tile, nhi, nlo, shift_ref, x_ref, cell_ref, v_ref, mean_ref, axis0_ref, axis1_ref,
    acc, zbox, xbox, ybox, work, turned, faces, out_sem, in_sem
):
    acc[...] = jnp.zeros_like(acc)
    cy = x_ref.shape[2]

    def put(f, i, value):
        (axis0_ref, axis1_ref)[f][i * cy : (i + 1) * cy, :] = value

    def step(t, carry):
        at = pl.ds(pl.multiple_of(t * tile, tile), tile)
        acc[...] += hist_tile(cell_ref[0:1, at], rows3(v_ref, at), nhi, nlo)
        return carry

    transfer = shift_fields(
        (0, 1), 1, shift_ref, x_ref, put, zbox, xbox, ybox, work, turned, faces, (out_sem, in_sem)
    )
    beside_work(transfer, step, v_ref.shape[1] // tile)
    mean_of(acc, mean_ref, nhi)


def middle_kernel(
    tile, nhi, nlo, cell_ref, v_ref, mean_ref, axis_ref, next_ref, next_mean_ref, acc, table_ref
):
    acc[...] = jnp.zeros_like(acc)
    make_table(mean_ref, axis_ref, table_ref, nhi, nlo)

    def step(t, carry):
        at = pl.ds(pl.multiple_of(t * tile, tile), tile)
        new = collide_tile(cell_ref[0:1, at], rows3(v_ref, at), table_ref[...], nhi, nlo)
        for k in range(3):
            next_ref[k : k + 1, at] = new[k]
        acc[...] += hist_tile(cell_ref[1:2, at], new, nhi, nlo)
        return carry

    lax.fori_loop(0, v_ref.shape[1] // tile, step, 0)
    mean_of(acc, next_mean_ref, nhi)


def last_kernel(
    tile, nhi, nlo, units, shift_ref, x_ref, cell_ref, v_ref, mean_ref, axis_ref, dir_ref, slot_ref,
    place_ref, who_ref, weight_ref, drift_ref, out_ref, kept_ref, force_ref, moved, table_ref, seen,
    going, coming, pushes, pulls, zbox, xbox, ybox, work, turned, faces, out_sem, in_sem
):
    moved[...] = jnp.zeros_like(moved)
    make_table(mean_ref, axis_ref, table_ref, nhi, nlo)
    per = tile // 128

    def step(t, carry):
        at = pl.ds(pl.multiple_of(t * tile, tile), tile)
        new = collide_tile(cell_ref[1:2, at], rows3(v_ref, at), table_ref[...], nhi, nlo)
        code = dir_ref[0:1, at]
        stays = code == 0
        rows = []
        for k in range(3):
            kept_ref[k : k + 1, at] = jnp.where(stays, new[k], 0.0)
            rows.extend(halves(new[k]))
            for j in range(per):
                seen[k, pl.ds(t * per + j, 1), :] = new[k][:, j * 128 : (j + 1) * 128]
        mask = one_hot(code - 1, 16)
        moved[...] += lax.dot_general(
            spread(rows, mask), one_hot(slot_ref[0:1, at], CAP), NT, preferred_element_type=F32
        )
        return carry

    def put(f, i, value):
        out_ref[f, i] = value

    sems = (out_sem, in_sem)
    rows_of_shift = [shift_ref.shape[0] - 1] * x_ref.shape[0]
    transfer = shift_fields(
        rows_of_shift, -1, shift_ref, x_ref, put, zbox, xbox, ybox, work, turned, faces, sems
    )
    particles = v_ref.shape[1]
    beside_work(transfer, step, particles // tile)
    for d in range(6):
        for k in range(3):
            going[d, k : k + 1, :] = (
                moved[32 * k + d : 32 * k + d + 1] + moved[32 * k + 16 + d : 32 * k + 17 + d]
            )
    copies = [
        send(going.at[d], coming.at[d], sems, 6 + d, AXES[d // 2], 1 - 2 * (d % 2)) for d in range(6)
    ]

    contacts = who_ref.shape[1]
    chunk = min(512, contacts)
    groups = seen.shape[1]
    sums = jnp.zeros((8 * 16, units), F32)
    parts = [halves(seen[k]) for k in range(3)]
    book = jnp.concatenate([jnp.concatenate(p, axis=1) for p in parts], axis=0)
    for c in range(contacts // chunk):
        at = slice(c * chunk, (c + 1) * chunk)
        hi, lo = split_index(who_ref[0:1, at], 128)
        hot = one_hot(lo, 128)
        got = jnp.dot(book, jnp.concatenate([hot, hot], axis=0), preferred_element_type=F32)
        here = lax.broadcasted_iota(jnp.int32, (groups, chunk), 0) == hi
        weight = weight_ref[0:1, at]
        rows = []
        for k in range(3):
            mine = jnp.where(here, got[k * groups : (k + 1) * groups], 0.0)
            rows.extend(halves(weight * jnp.sum(mine, axis=0, keepdims=True)))
        rows.extend(halves(weight))
        code, member = split_index(place_ref[0:1, at], units)
        sums = sums + lax.dot_general(
            spread(rows, one_hot(code, 16)), one_hot(member, units), NT, preferred_element_type=F32
        )
    totals = [sums[32 * k : 32 * k + 16] + sums[32 * k + 16 : 32 * k + 32] for k in range(4)]
    total = jnp.concatenate([t[6:7] for t in totals], axis=0)
    for d in range(6):
        for k in range(4):
            pushes[d, k : k + 1, :] = totals[k][d : d + 1]
    more = [
        send(pushes.at[d], pulls.at[d], sems, 12 + d, AXES[d // 2], 1 - 2 * (d % 2)) for d in range(6)
    ]
    for d, copy in enumerate(copies):
        copy.wait()
        kept_ref[:, particles + d * CAP : particles + (d + 1) * CAP] = coming[d, 0:3]
    for d, copy in enumerate(more):
        copy.wait()
        total = total + pulls[d]
    sum_w = total[3:4]
    force_ref[...] = (total[0:3] - sum_w * drift_ref[...]) / jnp.maximum(sum_w, 1.0)


AXES = ("gx", "gy", "gz")
MESH = pl.DeviceIdType.MESH


def beside(axis, sign):
    count = lax.axis_size(axis)
    return {axis: lax.rem(lax.axis_index(axis) + (sign + count), count)}


def greet():
    for axis in AXES:
        for sign in (1, -1):
            pl.semaphore_signal(
                pltpu.get_barrier_semaphore(), inc=1, device_id=beside(axis, sign), device_id_type=MESH
            )


def send(src, dst, sems, number, axis, sign):
    copy = pltpu.make_async_remote_copy(
        src_ref=src, dst_ref=dst, send_sem=sems[0].at[number], recv_sem=sems[1].at[number],
        device_id=beside(axis, sign), device_id_type=MESH,
    )
    copy.start()
    return copy


def both(pair, box, sems, number, axis):
    return [
        send(pair[0], box.at[0], sems, number, axis, -1),
        send(pair[1], box.at[1], sems, number + 1, axis, 1),
    ]


def shift_fields(rows, flip, shift_ref, x_ref, put, zbox, xbox, ybox, work, turned, faces, sems):
    n, cx, cy, nz = x_ref.shape
    ups = [[shift_ref[r, dim] * flip > 0 for dim in range(3)] for r in rows]
    greet()
    yield
    pl.semaphore_wait(pltpu.get_barrier_semaphore(), 6)
    copies = both((x_ref, x_ref), zbox, sems, 0, "gz")
    yield
    for copy in copies:
        copy.wait()
    for f in range(n):
        x = x_ref[f]
        plus = jnp.concatenate([x[:, :, 1:], zbox[0, f][:, :, 0:1]], axis=2)
        minus = jnp.concatenate([zbox[1, f][:, :, nz - 1 :], x[:, :, : nz - 1]], axis=2)
        work[f] = jnp.where(ups[f][2], plus, minus)
    copies = both((work.at[:, 0], work.at[:, cx - 1]), xbox, sems, 2, "gx")
    yield
    for copy in copies:
        copy.wait()
    for f in range(n):
        for i in range(cx):
            plus = work[f, i + 1] if i + 1 < cx else xbox[0, f]
            minus = work[f, i - 1] if i > 0 else xbox[1, f]
            row = jnp.where(ups[f][0], plus, minus)
            turned[f, i] = row
            faces[0, f, i : i + 1, :] = row[0:1]
            faces[1, f, i : i + 1, :] = row[cy - 1 :]
    copies = both((faces.at[0], faces.at[1]), ybox, sems, 4, "gy")
    yield
    for copy in copies:
        copy.wait()
    for f in range(n):
        for i in range(cx):
            x = turned[f, i]
            plus = jnp.concatenate([x[1:], ybox[0, f, i : i + 1, :]], axis=0)
            minus = jnp.concatenate([ybox[1, f, i : i + 1, :], x[: cy - 1]], axis=0)
            put(f, i, jnp.where(ups[f][1], plus, minus))


def shift_scratch(shape, kind):
    n, cx, cy, nz = shape
    return [
        pltpu.VMEM((2, n, cx, cy, nz), kind), pltpu.VMEM((2, n, cy, nz), kind),
        pltpu.VMEM((2, n, cx, nz), kind), pltpu.VMEM((n, cx, cy, nz), kind),
        pltpu.VMEM((n, cx, cy, nz), kind), pltpu.VMEM((2, n, cx, nz), kind),
    ]


def beside_work(transfer, step, tiles):
    for part in range(4):
        next(transfer)
        lax.fori_loop(tiles * part // 4, tiles * (part + 1) // 4, step, 0)
    for _ in transfer:
        pass


def contact_places(contact_colloid, units):
    size_x, size_y, size_z = (lax.axis_size(a) for a in ("gx", "gy", "gz"))
    mine_x, mine_y, mine_z = (lax.axis_index(a) for a in ("gx", "gy", "gz"))
    owner = contact_colloid // units
    apart_x = (owner // (size_y * size_z) - mine_x) % size_x
    apart_y = (owner // size_z % size_y - mine_y) % size_y
    apart_z = (owner % size_z - mine_z) % size_z
    code = jnp.full(owner.shape, 6, jnp.int32)
    for number, (apart, to) in reversed(
        list(
            enumerate(
                (
                    (apart_x, 1), (apart_x, size_x - 1), (apart_y, 1),
                    (apart_y, size_y - 1), (apart_z, 1), (apart_z, size_z - 1),
                )
            )
        )
    ):
        code = jnp.where(apart == to, number, code)
    return code * units + contact_colloid % units


def body(
    velocities, particle_cells, grid_shift, axis_index, migrate_dir, migrate_slot,
    contact_colloid, contact_particle, contact_weight, colloid_velocity,
):
    _, cx, cy, nlo = axis_index.shape
    nhi = cx * cy
    particles = velocities.shape[1]
    units = colloid_velocity.shape[1]
    tile = math.gcd(particles, TILE)
    mean_shape = jax.ShapeDtypeStruct((3, nhi, nlo), F32)
    acc = pltpu.VMEM((7 * nhi, nlo), F32)
    table = pltpu.VMEM((4 * nhi, 2 * nlo), BF)
    vmem = pl.BlockSpec(memory_space=pltpu.VMEM)
    smem = pl.BlockSpec(memory_space=pltpu.SMEM)

    def call(kernel, outs, scratch, number, *args):
        extra = {} if number is None else dict(collective_id=number, has_side_effects=True)
        first = vmem if number is None else smem
        return pl.pallas_call(
            functools.partial(kernel, tile, nhi, nlo),
            out_shape=outs,
            in_specs=[first] + [vmem] * (len(args) - 1),
            out_specs=tuple([vmem] * len(outs)),
            scratch_shapes=scratch,
            compiler_params=pltpu.CompilerParams(vmem_limit_bytes=48 * 2**20, **extra),
            cost_estimate=pl.CostEstimate(flops=10**9, bytes_accessed=30_000_000, transcendentals=0),
        )(*args)

    def semaphores(count):
        return [pltpu.SemaphoreType.DMA((count,)), pltpu.SemaphoreType.DMA((count,))]

    places = contact_places(contact_colloid, units)
    numbers = jax.ShapeDtypeStruct((nhi, nlo), jnp.int32)
    mean0, axis0, axis1 = call(
        first_kernel, (mean_shape, numbers, numbers),
        [acc] + shift_scratch(axis_index.shape, jnp.int32) + semaphores(6), 0,
        grid_shift, axis_index, particle_cells, velocities,
    )
    v1, mean1 = call(
        middle_kernel, (jax.ShapeDtypeStruct(velocities.shape, F32), mean_shape), [acc, table], None,
        particle_cells, velocities, mean0, axis0,
    )
    grid_mean = mean1.reshape(3, cx, cy, nlo)
    return call(
        lambda t, h, l, *refs: last_kernel(t, h, l, units, *refs),
        (
            jax.ShapeDtypeStruct(grid_mean.shape, F32),
            jax.ShapeDtypeStruct((3, particles + 6 * CAP), F32),
            jax.ShapeDtypeStruct((3, units), F32),
        ),
        [pltpu.VMEM((96, CAP), F32), table, pltpu.VMEM((3, particles // 128, 128), F32)]
        + [pltpu.VMEM((6, 3, CAP), F32)] * 2
        + [pltpu.VMEM((6, 4, units), F32)] * 2
        + shift_scratch(grid_mean.shape, F32)
        + semaphores(18),
        1,
        grid_shift, grid_mean, particle_cells, v1, mean1, axis1, migrate_dir.reshape(1, -1),
        migrate_slot.reshape(1, -1), places.reshape(1, -1), contact_particle.reshape(1, -1),
        contact_weight.reshape(1, -1), colloid_velocity,
    )


def solution(mesh):
    flat = P(None, ("gx", "gy", "gz"))
    line = P(("gx", "gy", "gz"))
    grid = P(None, "gx", "gy", "gz")
    return jax.shard_map(
        body,
        mesh=mesh,
        in_specs=(flat, flat, P(), grid, line, line, line, line, line, flat),
        out_specs=(grid, flat, flat),
        check_vma=False,
    )
```

profile of v0, /device:TPU:0, one launch (start us, length us, event | category | flops | bytes accessed | tf_op | source)
XLA Modules:
  0.0 56.2 jit_solution(14977369665164153117)
XLA Ops:
  0.6 0.0 copy-start.11
  0.6 0.0 copy-start.6
  0.7 0.7 %copy-done.11 = s32[2048]{0:T(1024)S(1)} copy-done((s32[2048]{0:T(1024)S(1)}, s32[2048]{0:T(1024)}, u32[]{:S(2)}) %copy-start.11) | copy-done | bytes 8216
  1.4 0.0 copy-start.10
  1.4 0.0 copy-done.6
  1.4 0.7 %copy-done.10 = s32[2,3]{1,0:T(2,128)S(1)} copy-done((s32[2,3]{1,0:T(2,128)S(1)}, s32[2,3]{1,0:T(2,128)}, u32[]{:S(2)}) %copy-start.10) | copy-done | bytes 48
  2.1 0.0 copy-start
  2.1 1.1 %copy-done = f32[3,40960]{1,0:T(4,128)S(1)} copy-done((f32[3,40960]{1,0:T(4,128)S(1)}, f32[3,40960]{1,0:T(4,128)}, u32[]{:S(2)}) %copy-start) | copy-done | bytes 491544
  3.1 0.0 copy-start.2
  3.2 1.0 %copy-done.2 = s32[2,40960]{1,0:T(2,128)S(1)} copy-done((s32[2,40960]{1,0:T(2,128)S(1)}, s32[2,40960]{1,0:T(2,128)}, u32[]{:S(2)}) %copy-start.2) | copy-done | bytes 327704
  4.1 0.0 copy-start.1
  4.1 15.0 %shard_map.121 = (f32[3,32,128]{2,1,0:T(8,128)S(1)}, s32[32,128]{1,0:T(8,128)S(1)}, s32[32,128]{1,0:T(8,128)S(1)}) custom-call(s32[2,3]{1,0:T(2,128)S(1)} %copy-done.10, s32[2,4,8,128]{3,2,1,0:T(8,128)S(1)} %copy-done.6, s32[2,40960]{1,0:T(2,128)S(1)} %copy-done.2, f32[3,40960]{1,0:T(4,128)S(1)} %copy-done), custom_call_target="tpu_custom_call" | custom-call | flops 1000000000 | bytes 30000000 | tf_op jit(solution)/shard_map/pallas_call | solution.py:355
  19.1 0.0 copy-done.1
  19.2 0.0 copy-start.3
  19.2 0.0 copy-start.4
  19.2 0.0 copy-start.5
  19.2 0.0 copy-start.7
  19.2 0.0 copy-start.8
  19.2 13.8 %shard_map.122 = (f32[3,40960]{1,0:T(4,128)S(1)}, f32[3,32,128]{2,1,0:T(8,128)S(1)}) custom-call(s32[2,40960]{1,0:T(2,128)S(1)} %copy-done.2, f32[3,40960]{1,0:T(4,128)S(1)} %copy-done.1, f32[3,32,128]{2,1,0:T(8,128)S(1)} %get-tuple-element.8.mean_ref, s32[32,128]{1,0:T(8,128)S(1)} %get-tuple-element.9.axis_ref), custom_call_target="tpu_custom_call" | custom-call | flops 1000000000 | bytes 30000000 | tf_op jit(solution)/shard_map/pallas_call | solution.py:355
  33.0 0.0 copy-start.9
  33.0 0.0 copy-done.3
  33.0 0.0 copy-done.4
  33.0 0.0 copy-done.5
  33.0 0.0 copy-done.7
  33.1 0.0 copy-done.8
  33.1 0.6 %copy-done.9 = f32[3,256]{1,0:T(4,128)S(1)} copy-done((f32[3,256]{1,0:T(4,128)S(1)}, f32[3,256]{1,0:T(4,128)}, u32[]{:S(2)}) %copy-start.9) | copy-done | bytes 3096
  33.7 20.4 %shard_map.123 = (f32[3,4,8,128]{3,2,1,0:T(8,128)S(1)}, f32[3,41920]{1,0:T(4,128)S(1)}, f32[3,256]{1,0:T(4,128)S(1)}) custom-call(s32[2,3]{1,0:T(2,128)S(1)} %copy-done.10, f32[3,4,8,128]{3,2,1,0:T(8,128)S(1)} %bitcast.11, s32[2,40960]{1,0:T(2,128)S(1)} %copy-done.3, f32[3,40960]{1,0:T(4,128)S(1)} %get-tuple-element.11.refs_3_, ...), custom_call_target="tpu_custom_call" | custom-call | flops 1000000000 | bytes 30000000 | tf_op jit(solution)/shard_map/pallas_call | solution.py:355
  54.1 0.6 %copy.16 = f32[3,4,8,128]{3,2,1,0:T(8,128)} copy(f32[3,4,8,128]{3,2,1,0:T(8,128)S(1)} %get-tuple-element.16) | data formatting | bytes 98304
  54.7 0.8 %copy.17 = f32[3,41920]{1,0:T(4,128)} copy(f32[3,41920]{1,0:T(4,128)S(1)} %get-tuple-element.17) | data formatting | bytes 1006080
  55.6 0.6 %copy.18 = f32[3,256]{1,0:T(4,128)} copy(f32[3,256]{1,0:T(4,128)S(1)} %get-tuple-element.18) | data formatting | bytes 6144
  (1 shorter events, 0.0 us)
Async XLA Ops:
  0.6 0.7 %copy-start.11 = (s32[2048]{0:T(1024)S(1)}, s32[2048]{0:T(1024)}, u32[]{:S(2)}) copy-start(s32[2048]{0:T(1024)} %param.16) | copy-start | bytes 24580
  0.6 0.8 %copy-start.6 = (s32[2,4,8,128]{3,2,1,0:T(8,128)S(1)}, s32[2,4,8,128]{3,2,1,0:T(8,128)}, u32[]{:S(2)}) copy-start(s32[2,4,8,128]{3,2,1,0:T(8,128)} %x_ref.1) | copy-start | bytes 98308
  1.4 0.7 %copy-start.10 = (s32[2,3]{1,0:T(2,128)S(1)}, s32[2,3]{1,0:T(2,128)}, u32[]{:S(2)}) copy-start(s32[2,3]{1,0:T(2,128)} %refs_0_.1) | copy-start | bytes 76
  2.1 1.1 %copy-start = (f32[3,40960]{1,0:T(4,128)S(1)}, f32[3,40960]{1,0:T(4,128)}, u32[]{:S(2)}) copy-start(f32[3,40960]{1,0:T(4,128)} %v_ref.3) | copy-start | bytes 1474564
  3.1 1.0 %copy-start.2 = (s32[2,40960]{1,0:T(2,128)S(1)}, s32[2,40960]{1,0:T(2,128)}, u32[]{:S(2)}) copy-start(s32[2,40960]{1,0:T(2,128)} %refs_2_.1) | copy-start | bytes 983044
  4.1 15.0 %copy-start.1 = (f32[3,40960]{1,0:T(4,128)S(1)}, f32[3,40960]{1,0:T(4,128)}, u32[]{:S(2)}) copy-start(f32[3,40960]{1,0:T(4,128)} %v_ref.3) | copy-start | bytes 1474564
  19.2 13.9 %copy-start.3 = (s32[2,40960]{1,0:T(2,128)S(1)}, s32[2,40960]{1,0:T(2,128)}, u32[]{:S(2)}) copy-start(s32[2,40960]{1,0:T(2,128)} %refs_2_.1) | copy-start | bytes 983044
  19.2 13.9 %copy-start.4 = (s32[40960]{0:T(1024)S(1)}, s32[40960]{0:T(1024)}, u32[]{:S(2)}) copy-start(s32[40960]{0:T(1024)} %param.14) | copy-start | bytes 491524
  19.2 13.9 %copy-start.5 = (s32[40960]{0:T(1024)S(1)}, s32[40960]{0:T(1024)}, u32[]{:S(2)}) copy-start(s32[40960]{0:T(1024)} %param.15) | copy-start | bytes 491524
  19.2 13.9 %copy-start.7 = (s32[2048]{0:T(1024)S(1)}, s32[2048]{0:T(1024)}, u32[]{:S(2)}) copy-start(s32[2048]{0:T(1024)} %param.17) | copy-start | bytes 24580
  19.2 13.9 %copy-start.8 = (f32[2048]{0:T(1024)S(1)}, f32[2048]{0:T(1024)}, u32[]{:S(2)}) copy-start(f32[2048]{0:T(1024)} %param.18) | copy-start | bytes 24580
  33.0 0.7 %copy-start.9 = (f32[3,256]{1,0:T(4,128)S(1)}, f32[3,256]{1,0:T(4,128)}, u32[]{:S(2)}) copy-start(f32[3,256]{1,0:T(4,128)} %refs_11_.1) | copy-start | bytes 9220
where the time goes:
time: 56.5 us; the launch traced here: 56.2 us
  Pallas kernels  49.2 us (87%)
  local copies, waits for them, and re-layouts  6.14 us (11%)
  between operations  0.78 us (1%)
    pallas_call x3, Pallas kernels, call(): pl.pallas_call(functools.partial(kernel, tile, nhi, nlo), out_shape=outs,...  49.2 us
    unnamed x27, local copies, waits for them, and re-layouts  6.14 us

commit v1 on v0

v1 whole, which is shorter than its diff:
```python
import functools
import math

import jax
import jax.numpy as jnp
from jax import lax
from jax.experimental import pallas as pl
from jax.experimental.pallas import tpu as pltpu
from jax.sharding import PartitionSpec as P

CAP = 160
ANGLE = 130.0 * math.pi / 180.0
COS, SIN = math.cos(ANGLE), math.sin(ANGLE)
NT = (((1,), (1,)), ((), ()))
BF = jnp.bfloat16
F8 = jnp.float8_e4m3fn
F32 = jnp.float32
I32 = jnp.int32
HI, LO = 16, 256
PLANES = 10
PRE = 8.0
SLOT = 64
TOP = 1 << 19
AXES = ("gx", "gy", "gz")
MESH = pl.DeviceIdType.MESH


def split_index(c, low):
    if low & (low - 1) == 0:
        return c >> (low.bit_length() - 1), c & (low - 1)
    return c // low, c % low


def one():
    return jnp.ones((), BF)


def zero():
    return jnp.zeros((), BF)


def one_hot(row, count):
    kind = BF if count <= 256 else F32
    wide = lax.broadcasted_iota(I32, (count, row.shape[1]), 0).astype(F32).astype(kind)
    return jnp.where(wide == row.astype(F32).astype(kind), jnp.ones((), kind), jnp.zeros((), kind)).astype(BF)


def halves(x):
    high = x.astype(BF)
    return high, (x - high.astype(F32)).astype(BF)


def spread(rows, mask):
    return jnp.concatenate([mask * row for row in rows], axis=0)


def row_at(ref, plane, j, rows):
    return jnp.broadcast_to(ref[plane, j : j + 1], (rows, 128)).astype(BF)


def iotas(count):
    return [(lax.broadcasted_iota(I32, (16, 128), 0) + 16 * i).astype(F32).astype(BF) for i in range(count // 16)]


def pieces(x):
    x = x * PRE
    a = x.astype(F8).astype(F32)
    r = (x - a) * 16.0
    b = r.astype(F8).astype(F32)
    s = (r - b) * 16.0
    return a, b, s.astype(F8).astype(F32)


def stage_hist(st, cell, v):
    st[0] = ((cell & 127) | ((cell >> 11) << 7)).astype(F32)
    st[1] = ((cell >> 7) & 15).astype(F32)
    for k in range(3):
        for i, piece in enumerate(pieces(v[k])):
            st[2 + 3 * k + i] = piece


def hist_group(st, j, steps):
    low, high = row_at(st, 0, j, 16), row_at(st, 1, j, 16)
    hot = []
    for i in range(LO // 32):
        pair = [jnp.where(steps[2 * i + k] == low, one(), zero()) for k in range(2)]
        hot.append(jnp.concatenate(pair, axis=0).astype(F8))
    here = steps[0] == high
    rows = [jnp.where(here, row_at(st, 2 + q, j, 16), zero()) for q in range(PLANES - 1)]
    rows.append(jnp.where(here, one(), zero()))
    left = [jnp.concatenate(rows[2 * i : 2 * i + 2], axis=0).astype(F8) for i in range(PLANES // 2)]
    return jnp.concatenate(hot, axis=0), jnp.concatenate(left, axis=0)


def hist_add(acc, st, tiles, steps):
    groups = [hist_group(st.at[u], j, steps) for u in tiles for j in range(8)]
    left = jnp.concatenate([g[1] for g in groups], axis=1)
    hot = jnp.concatenate([g[0] for g in groups], axis=1)
    acc[...] += lax.dot_general(left, hot, NT, preferred_element_type=F32)


def mean_of(total, mean_ref):
    def plane(q):
        x = total[q * HI : (q + 1) * HI]
        return jnp.concatenate([x[:, :128], x[:, 128:]], axis=0)

    count = jnp.maximum(plane(9), 1.0)
    for k in range(3):
        sums = plane(3 * k) + plane(3 * k + 1) * (1.0 / 16) + plane(3 * k + 2) * (1.0 / 256)
        mean_ref[k] = sums * (1.0 / PRE) / count


def signs_of(index):
    return [jnp.where((index & (1 << i)) != 0, 1.0, -1.0) for i in range(3)]


def rotate(e, v):
    along = ((1.0 - COS) / 3.0) * (e[0] * v[0] + e[1] * v[1] + e[2] * v[2])
    turn = SIN / math.sqrt(3.0)
    out = []
    for i in range(3):
        j, k = (i + 1) % 3, (i + 2) % 3
        out.append(COS * v[i] + e[i] * along + turn * (e[j] * v[k] - e[k] * v[j]))
    return out


def make_table(mean_ref, axis_ref, table_ref, unit_ref):
    mean = [mean_ref[k] for k in range(3)]
    index = axis_ref[...]
    turned = rotate(signs_of(index), mean)
    offset = [mean[k] - turned[k] for k in range(3)]
    most = jnp.maximum(jnp.maximum(jnp.abs(offset[0]), jnp.abs(offset[1])), jnp.abs(offset[2]))
    most = jnp.max(jnp.max(most, axis=0, keepdims=True), axis=1, keepdims=True)
    most = jnp.maximum(most, 1e-25)
    scale = (TOP - 2.0) / most
    q = []
    for k in range(3):
        x = offset[k] * scale
        q.append((x + jnp.where(x >= 0.0, 0.5, -0.5)).astype(I32))
    last = q[2] + TOP
    table_ref[0] = (q[0] << 12) | (last >> 8)
    table_ref[1] = (q[1] << 12) | ((last & 255) << 4) | index
    unit_ref[...] = jnp.broadcast_to(most * (1.0 / (TOP - 2.0)), (8, 128))


def look_up(table_ref, cell):
    lane = cell & 127
    depth = table_ref.shape[1].bit_length() - 1
    bits = [(cell & (1 << (7 + b))) != 0 for b in range(depth)]

    def pick(word, b, at):
        if b < 0:
            row = jnp.broadcast_to(table_ref[word, at : at + 1], (8, 128))
            return jnp.take_along_axis(row, lane, axis=1, mode="promise_in_bounds")
        return jnp.where(bits[b], pick(word, b - 1, at + (1 << b)), pick(word, b - 1, at))

    return pick(0, depth - 1, 0), pick(1, depth - 1, 0)


def collide(table_ref, unit, cell, v):
    a, b = look_up(table_ref, cell)
    last = (((a & 4095) << 8) | ((b >> 4) & 255)) - TOP
    offset = [(x.astype(F32)) * unit for x in (a >> 12, b >> 12, last)]
    turned = rotate(signs_of(b), v)
    return [turned[k] + offset[k] for k in range(3)]


def beside(axis, sign):
    count = lax.axis_size(axis)
    return {axis: lax.rem(lax.axis_index(axis) + (sign + count), count)}


def greet():
    for axis in AXES:
        for sign in (1, -1):
            pl.semaphore_signal(
                pltpu.get_barrier_semaphore(), inc=1, device_id=beside(axis, sign), device_id_type=MESH
            )


def send(src, dst, sems, number, axis, sign):
    copy = pltpu.make_async_remote_copy(
        src_ref=src, dst_ref=dst, send_sem=sems[0].at[number], recv_sem=sems[1].at[number],
        device_id=beside(axis, sign), device_id_type=MESH,
    )
    copy.start()
    return copy


def both(pair, box, sems, number, axis):
    return [
        send(pair[0], box.at[0], sems, number, axis, -1),
        send(pair[1], box.at[1], sems, number + 1, axis, 1),
    ]


def shift_fields(rows, flip, shift_ref, x_ref, put, boxes, sems, first, before):
    zbox, xbox, ybox, work, turned, faces = boxes
    n, cx, cy, nz = x_ref.shape
    ups = [[shift_ref[r, dim] * flip > 0 for dim in range(3)] for r in rows]
    yield
    before()
    copies = both((x_ref, x_ref), zbox, sems, first, "gz")
    yield
    for copy in copies:
        copy.wait()
    for f in range(n):
        x = x_ref[f]
        plus = jnp.concatenate([x[:, :, 1:], zbox[0, f][:, :, 0:1]], axis=2)
        minus = jnp.concatenate([zbox[1, f][:, :, nz - 1 :], x[:, :, : nz - 1]], axis=2)
        work[f] = jnp.where(ups[f][2], plus, minus)
    copies = both((work.at[:, 0], work.at[:, cx - 1]), xbox, sems, first + 2, "gx")
    yield
    for copy in copies:
        copy.wait()
    for f in range(n):
        for i in range(cx):
            plus = work[f, i + 1] if i + 1 < cx else xbox[0, f]
            minus = work[f, i - 1] if i > 0 else xbox[1, f]
            row = jnp.where(ups[f][0], plus, minus)
            turned[f, i] = row
            faces[0, f, i : i + 1, :] = row[0:1]
            faces[1, f, i : i + 1, :] = row[cy - 1 :]
    copies = both((faces.at[0], faces.at[1]), ybox, sems, first + 4, "gy")
    yield
    for copy in copies:
        copy.wait()
    for f in range(n):
        for i in range(cx):
            x = turned[f, i]
            plus = jnp.concatenate([x[1:], ybox[0, f, i : i + 1, :]], axis=0)
            minus = jnp.concatenate([ybox[1, f, i : i + 1, :], x[: cy - 1]], axis=0)
            put(f, i, jnp.where(ups[f][1], plus, minus))


def shift_scratch(shape, kind):
    n, cx, cy, nz = shape
    return [
        pltpu.VMEM((2, n, cx, cy, nz), kind), pltpu.VMEM((2, n, cy, nz), kind),
        pltpu.VMEM((2, n, cx, nz), kind), pltpu.VMEM((n, cx, cy, nz), kind),
        pltpu.VMEM((n, cx, cy, nz), kind), pltpu.VMEM((2, n, cx, nz), kind),
    ]


def beside_work(transfer, step, count):
    for part in range(4):
        next(transfer)
        lax.fori_loop(count * part // 4, count * (part + 1) // 4, step, 0)
    for _ in transfer:
        pass


def contact_places(colloid, units):
    size_x, size_y, size_z = (lax.axis_size(a) for a in AXES)
    mine_x, mine_y, mine_z = (lax.axis_index(a) for a in AXES)
    owner, member = split_index(colloid, units)
    rest, own_z = split_index(owner, size_z)
    own_x, own_y = split_index(rest, size_y)

    def apart(own, mine, size):
        return split_index(own - mine + size, size)[1]

    apart_x, apart_y, apart_z = apart(own_x, mine_x, size_x), apart(own_y, mine_y, size_y), apart(own_z, mine_z, size_z)
    code = jnp.full(colloid.shape, 6, I32)
    pairs = (
        (apart_x, 1), (apart_x, size_x - 1), (apart_y, 1),
        (apart_y, size_y - 1), (apart_z, 1), (apart_z, size_z - 1),
    )
    for number, (gap, to) in reversed(list(enumerate(pairs))):
        code = jnp.where(gap == to, number, code)
    return code, member


def main_kernel(
    per, units, shift_ref, v_in, cs, axis_hbm, dir_hbm, slot_hbm, who_hbm, colloid_hbm, weight_hbm, drift_ref,
    kept_ref, tail_ref, cellv_ref, force_ref,
    vs, field, dirs, slots, who, colloid, weight, axes, mean, field_mean, table, unit_ref, st, acc, moved, book,
    going, coming, pushes, pulls, *rest
):
    boxes_a, boxes_b, (local_sem, out_sem, in_sem) = rest[:6], rest[6:12], rest[12:]
    sems = (out_sem, in_sem)
    cx, cy, nz = axis_hbm.shape[1:]
    groups = v_in.shape[1]
    loops = groups // (8 * per)

    def fetch(src, dst, number):
        copy = pltpu.make_async_copy(src, dst, local_sem.at[number])
        copy.start()
        return copy

    first = [fetch(axis_hbm, field, 0)]
    late = [fetch(dir_hbm, dirs, 1), fetch(slot_hbm, slots, 2), fetch(who_hbm, who, 3)]
    late += [fetch(colloid_hbm, colloid, 4), fetch(weight_hbm, weight, 5)]
    greet()

    steps = iotas(LO)

    def rows_of(t, u):
        return pl.ds(pl.multiple_of((t * per + u) * 8, 8), 8)

    def meet():
        pl.semaphore_wait(pltpu.get_barrier_semaphore(), 6)
        first[0].wait()

    def put_axis(f, i, value):
        axes[f, i * cy : (i + 1) * cy, :] = value

    acc[...] = jnp.zeros_like(acc)

    def step0(t, carry):
        for u in range(per):
            at = rows_of(t, u)
            stage_hist(st.at[u], cs[0, at], [v_in[k, at] for k in range(3)])
        hist_add(acc, st, range(per), steps)
        return carry

    transfer = shift_fields((0, 1), 1, shift_ref, field, put_axis, boxes_a, sems, 0, meet)
    beside_work(transfer, step0, loops)
    mean_of(acc[...], mean)
    for copy in late:
        copy.wait()
    make_table(mean, axes.at[0], table, unit_ref)
    acc[...] = jnp.zeros_like(acc)

    def step1(t, carry):
        unit = unit_ref[...]
        for u in range(per):
            at = rows_of(t, u)
            new = collide(table, unit, cs[0, at], [v_in[k, at] for k in range(3)])
            for k in range(3):
                vs[k, at] = new[k]
            stage_hist(st.at[u], cs[1, at], new)
        hist_add(acc, st, range(per), steps)
        return carry

    lax.fori_loop(0, loops, step1, 0)
    mean_of(acc[...], mean)
    make_table(mean, axes.at[1], table, unit_ref)
    for k in range(3):
        for i in range(cx):
            field_mean[k, i] = mean[k, i * cy : (i + 1) * cy]
    moved[...] = jnp.zeros_like(moved)
    narrow = iotas(SLOT)

    def leave_group(ref, j):
        low, high = row_at(ref, 0, j, 16), row_at(ref, 1, j, 16)
        hot = jnp.concatenate([jnp.where(wide == low, one(), zero()) for wide in narrow], axis=0)
        here = narrow[0] == high
        rows = [jnp.where(here, row_at(ref, 2 + q, j, 16), zero()) for q in range(6)]
        return hot, jnp.concatenate(rows, axis=0)

    def step2(t, carry):
        unit = unit_ref[...]
        hots, lefts = [], []
        for u in range(per):
            at = rows_of(t, u)
            new = collide(table, unit, cs[1, at], [vs[k, at] for k in range(3)])
            code = dirs[at]
            stays = code == 0
            goal = jnp.where(stays, -SLOT, (code - 1) * CAP + slots[at])
            st[u, 0] = (goal & (SLOT - 1)).astype(F32)
            st[u, 1] = (goal >> (SLOT.bit_length() - 1)).astype(F32)
            for k in range(3):
                kept_ref[k, at] = jnp.where(stays, new[k], 0.0)
                high, low = halves(new[k])
                st[u, 2 + 2 * k] = high.astype(F32)
                st[u, 3 + 2 * k] = low.astype(F32)
        for u in range(0, per, 2):
            at = pl.ds(pl.multiple_of((t * per + u) * 8, 16), 16)
            for k in range(3):
                for i in range(2):
                    both_tiles = jnp.concatenate([st[u, 2 + 2 * k + i], st[u + 1, 2 + 2 * k + i]], axis=0)
                    book[k, at, i * 128 : (i + 1) * 128] = both_tiles.astype(BF)
        for u in range(per):
            for j in range(8):
                hot, left = leave_group(st.at[u], j)
                hots.append(hot)
                lefts.append(left)
        moved[...] += lax.dot_general(
            jnp.concatenate(lefts, axis=1), jnp.concatenate(hots, axis=1), NT, preferred_element_type=F32
        )
        return carry

    def put_mean(f, i, value):
        cellv_ref[f, i] = value

    rows_of_shift = [shift_ref.shape[0] - 1] * 3
    transfer = shift_fields(
        rows_of_shift, -1, shift_ref, field_mean, put_mean, boxes_b, sems, 6, lambda: None
    )
    beside_work(transfer, step2, loops)

    for k in range(3):
        value = moved[32 * k : 32 * k + 16] + moved[32 * k + 16 : 32 * k + 32]
        for d in range(6):
            at, end, parts = d * CAP, (d + 1) * CAP, []
            while at < end:
                r, c = at // SLOT, at % SLOT
                size = min(SLOT - c, end - at)
                parts.append(value[r : r + 1, c : c + size])
                at += size
            going[d, k : k + 1, :] = jnp.concatenate(parts, axis=1)
    copies = [
        send(going.at[d], coming.at[d], sems, 12 + d, AXES[d // 2], 1 - 2 * (d % 2)) for d in range(6)
    ]

    contacts = who.shape[1]
    chunk = min(512, contacts)
    sums = jnp.zeros((8 * 16, units), F32)
    pages = book[...].reshape(3 * groups, 256)
    for c in range(contacts // chunk):
        at = slice(c * chunk, (c + 1) * chunk)
        hi, lo = split_index(who[0:1, at], 128)
        hot = one_hot(lo, 128)
        got = jnp.dot(pages, jnp.concatenate([hot, hot], axis=0), preferred_element_type=F32)
        here = lax.broadcasted_iota(I32, (groups, chunk), 0) == hi
        force = weight[0:1, at]
        rows = []
        for k in range(3):
            mine = jnp.where(here, got[k * groups : (k + 1) * groups], 0.0)
            rows.extend(halves(force * jnp.sum(mine, axis=0, keepdims=True)))
        rows.extend(halves(force))
        code, member = contact_places(colloid[0:1, at], units)
        sums = sums + lax.dot_general(
            spread(rows, one_hot(code, 16)), one_hot(member, units), NT, preferred_element_type=F32
        )
    totals = [sums[32 * k : 32 * k + 16] + sums[32 * k + 16 : 32 * k + 32] for k in range(4)]
    total = jnp.concatenate([x[6:7] for x in totals], axis=0)
    for d in range(6):
        for k in range(4):
            pushes[d, k : k + 1, :] = totals[k][d : d + 1]
    more = [
        send(pushes.at[d], pulls.at[d], sems, 18 + d, AXES[d // 2], 1 - 2 * (d % 2)) for d in range(6)
    ]
    for d, copy in enumerate(copies):
        copy.wait()
        for k in range(3):
            tail_ref[k, :, d * CAP : (d + 1) * CAP] = coming[d, k : k + 1]
    for d, copy in enumerate(more):
        copy.wait()
        total = total + pulls[d]
    sum_w = total[3:4]
    force_ref[...] = (total[0:3] - sum_w * drift_ref[...]) / jnp.maximum(sum_w, 1.0)


def last_kernel(kept_ref, tail_ref, cellv_ref, force_ref, cellv_hbm, out_hbm, force_hbm, sem):
    particles, extra = kept_ref.shape[2], tail_ref.shape[2]
    copies = []
    for k in range(3):
        row = pl.ds(k, 1)
        copies.append((kept_ref.at[k], out_hbm.at[row, pl.ds(0, particles)]))
        copies.append((tail_ref.at[k], out_hbm.at[row, pl.ds(particles, extra)]))
    copies += [(cellv_ref, cellv_hbm), (force_ref, force_hbm)]
    copies = [pltpu.make_async_copy(src, dst, sem.at[i]) for i, (src, dst) in enumerate(copies)]
    for copy in copies:
        copy.start()
    for copy in copies:
        copy.wait()


def body(
    velocities, particle_cells, grid_shift, axis_index, migrate_dir, migrate_slot,
    contact_colloid, contact_particle, contact_weight, colloid_velocity,
):
    _, cx, cy, nlo = axis_index.shape
    particles = velocities.shape[1]
    units = colloid_velocity.shape[1]
    contacts = contact_weight.shape[0]
    groups = particles // 128
    cells = (cx * cy, nlo)
    if cells != (2 * HI, 128) or particles % 4096 or 6 * CAP > 16 * SLOT:
        raise ValueError("sizes")
    per = 4
    grid_mean = (3, cx, cy, nlo)
    vmem = pl.BlockSpec(memory_space=pltpu.VMEM)
    smem = pl.BlockSpec(memory_space=pltpu.SMEM)
    hbm = pl.BlockSpec(memory_space=pl.ANY)
    outs = (
        jax.ShapeDtypeStruct((3, groups, 128), F32),
        jax.ShapeDtypeStruct((3, 1, 6 * CAP), F32),
        jax.ShapeDtypeStruct(grid_mean, F32),
        jax.ShapeDtypeStruct((3, units), F32),
    )
    dma = pltpu.SemaphoreType.DMA
    kept, tail, cellv, force = pl.pallas_call(
        functools.partial(main_kernel, per, units),
        out_shape=outs,
        in_specs=[smem] + [vmem] * 2 + [hbm] * 6 + [vmem],
        out_specs=(vmem,) * 4,
        scratch_shapes=[
            pltpu.VMEM((3, groups, 128), F32), pltpu.VMEM(axis_index.shape, I32), pltpu.VMEM((groups, 128), I32), pltpu.VMEM((groups, 128), I32),
            pltpu.VMEM((1, contacts), I32), pltpu.VMEM((1, contacts), I32), pltpu.VMEM((1, contacts), F32),
            pltpu.VMEM((2,) + cells, I32), pltpu.VMEM((3,) + cells, F32), pltpu.VMEM(grid_mean, F32),
            pltpu.VMEM((2,) + cells, I32), pltpu.VMEM((8, 128), F32), pltpu.VMEM((per, PLANES + 1, 8, 128), F32),
            pltpu.VMEM((PLANES * HI, LO), F32), pltpu.VMEM((96, SLOT), F32), pltpu.VMEM((3, groups, 256), BF),
            pltpu.VMEM((6, 3, CAP), F32), pltpu.VMEM((6, 3, CAP), F32),
            pltpu.VMEM((6, 4, units), F32), pltpu.VMEM((6, 4, units), F32),
        ]
        + shift_scratch(axis_index.shape, I32) + shift_scratch(grid_mean, F32)
        + [dma((6,)), dma((24,)), dma((24,))],
        compiler_params=pltpu.CompilerParams(
            vmem_limit_bytes=48 * 2**20, collective_id=0, has_side_effects=True
        ),
        cost_estimate=pl.CostEstimate(flops=10**9, bytes_accessed=30_000_000, transcendentals=0),
    )(
        grid_shift, velocities.reshape(3, groups, 128), particle_cells.reshape(2, groups, 128), axis_index, migrate_dir.reshape(groups, 128),
        migrate_slot.reshape(groups, 128), contact_particle.reshape(1, -1), contact_colloid.reshape(1, -1),
        contact_weight.reshape(1, -1), colloid_velocity,
    )
    return pl.pallas_call(
        last_kernel,
        out_shape=(
            jax.ShapeDtypeStruct(grid_mean, F32),
            jax.ShapeDtypeStruct((3, particles + 6 * CAP), F32),
            jax.ShapeDtypeStruct((3, units), F32),
        ),
        in_specs=[vmem] * 4,
        out_specs=(hbm,) * 3,
        scratch_shapes=[dma((8,))],
        compiler_params=pltpu.CompilerParams(vmem_limit_bytes=8 * 2**20),
    )(kept.reshape(3, 1, particles), tail, cellv, force)


def solution(mesh):
    flat = P(None, AXES)
    line = P(AXES)
    grid = P(None, *AXES)

    return jax.shard_map(
        body,
        mesh=mesh,
        in_specs=(flat, flat, P(), grid, line, line, line, line, line, flat),
        out_specs=(grid, flat, flat),
        check_vma=False,
    )
```

time: 56.5 us -> 42 us (0.74)
  Pallas kernels: 49.2 us -> 39 us
  local copies, waits for them, and re-layouts: 6.14 us -> 2.14 us
    pallas_call x3 -> x2, Pallas kernels: 49.2 us -> 39 us  [the longest x1 38.2 us: body(): pl.pallas_call(functools.partial(main_kernel, per, units), out_shape=outs...]
    unnamed x27 -> x20, local copies, waits for them, and re-layouts: 6.14 us -> 2.14 us
where the time goes in v1:
time: 42 us; the launch traced here: 41.9 us
  Pallas kernels  39 us (93%)
  local copies, waits for them, and re-layouts  2.14 us (5%)
  between operations  0.72 us (2%)
    pallas_call x1, Pallas kernels, body(): pl.pallas_call(functools.partial(main_kernel, per, units), out_shape=outs...  38.2 us
    unnamed x20, local copies, waits for them, and re-layouts  2.14 us
    pallas_call x1, Pallas kernels, body(): pl.pallas_call(last_kernel, out_shape=(jax.ShapeDtypeStruct(grid_mean, F3...  0.87 us

profile of v1, /device:TPU:0, one launch (start us, length us, event | category | flops | bytes accessed | tf_op | source)
XLA Modules:
  0.0 41.9 jit_solution(9592503396137413126)
XLA Ops:
  0.6 0.0 copy-start.8
  0.6 1.1 %copy.18 = s32[1,2,320,128]{3,2,1,0:T(8,128)S(1)} copy(s32[1,2,320,128]{3,1,2,0:T(2,128)} %bitcast.23) | data formatting | bytes 655360
  1.7 0.1 copy-done.8
  1.8 0.0 copy-start
  1.8 0.0 copy-start.1
  1.8 0.0 copy-start.2
  1.8 0.0 copy-start.3
  1.8 0.0 copy-start.4
  1.8 0.0 copy-start.5
  1.9 0.0 copy-start.6
  1.9 0.0 copy-start.7
  1.9 0.8 %copy-done = s32[40960]{0:T(1024)S(1)} copy-done((s32[40960]{0:T(1024)S(1)}, s32[40960]{0:T(1024)}, u32[]{:S(2)}) %copy-start) | copy-done | bytes 163864
  2.7 0.1 copy-done.1
  2.8 0.0 copy-done.2
  2.8 0.0 copy-done.3
  2.8 0.0 copy-done.4
  2.8 0.0 copy-done.5
  2.8 0.0 copy-done.6
  2.8 0.0 copy-done.7
  2.8 38.2 %shard_map.121 = (f32[3,320,128]{2,1,0:T(8,128)S(1)}, f32[3,1,960]{2,1,0:T(1,128)S(1)}, f32[3,4,8,128]{3,2,1,0:T(8,128)S(1)}, f32[3,256]{1,0:T(4,128)S(1)}) custom-call(s32[2,3]{1,0:T(2,128)S(1)} %copy-done.7, f32[3,320,128]{2,1,0:T(8,128)S(1)} %bitcast.15, s32[2,320,128]{2,1,0:T(8,128)S(1)} %bitcast.16, s32[2,4,8,128]{3,2,1,0:T(8,128)S(1)} %copy-done.2, ...), custom_call_target="tpu_custom_call" | custom-call | flops 1000000000 | bytes 30000000 | tf_op jit(solution)/shard_map/pallas_call | solution.py:485
  41.0 0.9 %shard_map.122 = (f32[3,4,8,128]{3,2,1,0:T(8,128)}, f32[3,41920]{1,0:T(4,128)}, f32[3,256]{1,0:T(4,128)}) custom-call(f32[3,1,40960]{2,1,0:T(1,128)S(1)} %bitcast.14, f32[3,1,960]{2,1,0:T(1,128)S(1)} %get-tuple-element.8.tail_ref, f32[3,4,8,128]{3,2,1,0:T(8,128)S(1)} %get-tuple-element.9.cellv_ref, f32[3,256]{1,0:T(4,128)S(1)} %get-tuple-element.10.force_ref), custom_call_target="tpu_custom_call" | custom-call | tf_op jit(solution)/shard_map/pallas_call | solution.py:510
  (1 shorter events, 0.0 us)
Async XLA Ops:
  0.6 1.2 %copy-start.8 = (f32[3,40960]{1,0:T(4,128)S(1)}, f32[3,40960]{1,0:T(4,128)}, u32[]{:S(2)}) copy-start(f32[3,40960]{1,0:T(4,128)} %param.10) | copy-start | bytes 1474564
  1.8 0.9 %copy-start = (s32[40960]{0:T(1024)S(1)}, s32[40960]{0:T(1024)}, u32[]{:S(2)}) copy-start(s32[40960]{0:T(1024)} %param.14) | copy-start | bytes 491524
  1.8 1.0 %copy-start.1 = (s32[40960]{0:T(1024)S(1)}, s32[40960]{0:T(1024)}, u32[]{:S(2)}) copy-start(s32[40960]{0:T(1024)} %param.15) | copy-start | bytes 491524
  1.8 1.0 %copy-start.2 = (s32[2,4,8,128]{3,2,1,0:T(8,128)S(1)}, s32[2,4,8,128]{3,2,1,0:T(8,128)}, u32[]{:S(2)}) copy-start(s32[2,4,8,128]{3,2,1,0:T(8,128)} %axis_hbm.1) | copy-start | bytes 98308
  1.8 1.0 %copy-start.3 = (s32[2048]{0:T(1024)S(1)}, s32[2048]{0:T(1024)}, u32[]{:S(2)}) copy-start(s32[2048]{0:T(1024)} %param.17) | copy-start | bytes 24580
  1.8 1.0 %copy-start.4 = (s32[2048]{0:T(1024)S(1)}, s32[2048]{0:T(1024)}, u32[]{:S(2)}) copy-start(s32[2048]{0:T(1024)} %param.16) | copy-start | bytes 24580
  1.8 1.0 %copy-start.5 = (f32[2048]{0:T(1024)S(1)}, f32[2048]{0:T(1024)}, u32[]{:S(2)}) copy-start(f32[2048]{0:T(1024)} %param.18) | copy-start | bytes 24580
  1.9 1.0 %copy-start.6 = (f32[3,256]{1,0:T(4,128)S(1)}, f32[3,256]{1,0:T(4,128)}, u32[]{:S(2)}) copy-start(f32[3,256]{1,0:T(4,128)} %drift_ref.1) | copy-start | bytes 9220
  1.9 0.9 %copy-start.7 = (s32[2,3]{1,0:T(2,128)S(1)}, s32[2,3]{1,0:T(2,128)}, u32[]{:S(2)}) copy-start(s32[2,3]{1,0:T(2,128)} %shift_ref.1) | copy-start | bytes 76

commit v2 on v1

--- a/solution.py
+++ b/solution.py
@@ -21,8 +21,10 @@
 PRE = 8.0
 SLOT = 64
 TOP = 1 << 19
+EARLY = 1
 AXES = ("gx", "gy", "gz")
 MESH = pl.DeviceIdType.MESH
+WAYS = [(x, y, z) for x in (-1, 0, 1) for y in (-1, 0, 1) for z in (-1, 0, 1) if (x, y, z) != (0, 0, 0)]
 
 
 def split_index(c, low):
@@ -170,12 +172,23 @@
     return {axis: lax.rem(lax.axis_index(axis) + (sign + count), count)}
 
 
+def kept_ways():
+    return [w for w in WAYS if w[2] >= 0 or lax.axis_size("gz") > 2]
+
+
 def greet():
-    for axis in AXES:
-        for sign in (1, -1):
-            pl.semaphore_signal(
-                pltpu.get_barrier_semaphore(), inc=1, device_id=beside(axis, sign), device_id_type=MESH
-            )
+    for way in kept_ways():
+        pl.semaphore_signal(
+            pltpu.get_barrier_semaphore(), inc=1, device_id=towards(way), device_id_type=MESH
+        )
+
+
+def towards(way):
+    target = {}
+    for axis, sign in zip(AXES, way):
+        if sign:
+            target.update(beside(axis, sign))
+    return target
 
 
 def send(src, dst, sems, number, axis, sign):
@@ -187,67 +200,77 @@
     return copy
 
 
-def both(pair, box, sems, number, axis):
-    return [
-        send(pair[0], box.at[0], sems, number, axis, -1),
-        send(pair[1], box.at[1], sems, number + 1, axis, 1),
-    ]
-
-
-def shift_fields(rows, flip, shift_ref, x_ref, put, boxes, sems, first, before):
-    zbox, xbox, ybox, work, turned, faces = boxes
+def start_shift(x_ref, boxes, sems, first):
+    zbox, xbox, ybox, faces = boxes
+    n, cx, cy, _ = x_ref.shape
+    for f in range(n):
+        for i in range(cx):
+            faces[0, f, i : i + 1, :] = x_ref[f, i, 0:1]
+            faces[1, f, i : i + 1, :] = x_ref[f, i, cy - 1 : cy]
+    copies = []
+    for number, way in enumerate(kept_ways()):
+        x, y, z = way
+        if y:
+            src, dst = faces.at[0 if y > 0 else 1], ybox.at[x + 1, 0 if y > 0 else 1, z + 1]
+        elif x:
+            src, dst = x_ref.at[:, 0 if x > 0 else cx - 1], xbox.at[0 if x > 0 else 1, z + 1]
+        else:
+            src, dst = x_ref, zbox.at[0 if z > 0 else 1]
+        copy = pltpu.make_async_remote_copy(
+            src_ref=src, dst_ref=dst, send_sem=sems[0].at[first + number], recv_sem=sems[1].at[first + number],
+            device_id=towards((-x, -y, -z)), device_id_type=MESH,
+        )
+        copy.start()
+        copies.append(copy)
+    return copies
+
+
+def finish_shift(copies, rows, flip, shift_ref, x_ref, boxes, put):
+    zbox, xbox, ybox, _ = boxes
     n, cx, cy, nz = x_ref.shape
-    ups = [[shift_ref[r, dim] * flip > 0 for dim in range(3)] for r in rows]
-    yield
-    before()
-    copies = both((x_ref, x_ref), zbox, sems, first, "gz")
-    yield
+    deep = lax.axis_size("gz") > 2
+    levels = (0, 1, 2) if deep else (2, 1, 2)
     for copy in copies:
         copy.wait()
     for f in range(n):
-        x = x_ref[f]
-        plus = jnp.concatenate([x[:, :, 1:], zbox[0, f][:, :, 0:1]], axis=2)
-        minus = jnp.concatenate([zbox[1, f][:, :, nz - 1 :], x[:, :, : nz - 1]], axis=2)
-        work[f] = jnp.where(ups[f][2], plus, minus)
-    copies = both((work.at[:, 0], work.at[:, cx - 1]), xbox, sems, first + 2, "gx")
-    yield
-    for copy in copies:
-        copy.wait()
-    for f in range(n):
+        up_x, up_y, up_z = (shift_ref[rows[f], dim] * flip > 0 for dim in range(3))
+
+        def turn(parts):
+            low, mid, high = parts
+            end = mid.ndim - 1
+            cut = lambda v, at, to: lax.slice_in_dim(v, at, to, axis=end)
+            plus = jnp.concatenate([cut(mid, 1, nz), cut(high, 0, 1)], axis=end)
+            minus = jnp.concatenate([cut(low, nz - 1, nz), cut(mid, 0, nz - 1)], axis=end)
+            return jnp.where(up_z, plus, minus)
+
+        def edge(z):
+            pick = [
+                jnp.where(up_x, ybox[2, s, z, f, 0:1], ybox[0, s, z, f, cx - 1 : cx]) for s in range(2)
+            ]
+            return jnp.where(up_y, pick[0], pick[1])
+
+        core = turn([zbox[1 if deep else 0, f], x_ref[f], zbox[0, f]])
+        side = turn([jnp.where(up_x, xbox[0, z, f], xbox[1, z, f]) for z in levels])
+        face = turn([jnp.where(up_y, ybox[1, 0, z, f], ybox[1, 1, z, f]) for z in levels])
+        corner = turn([edge(z) for z in levels])
         for i in range(cx):
-            plus = work[f, i + 1] if i + 1 < cx else xbox[0, f]
-            minus = work[f, i - 1] if i > 0 else xbox[1, f]
-            row = jnp.where(ups[f][0], plus, minus)
-            turned[f, i] = row
-            faces[0, f, i : i + 1, :] = row[0:1]
-            faces[1, f, i : i + 1, :] = row[cy - 1 :]
-    copies = both((faces.at[0], faces.at[1]), ybox, sems, first + 4, "gy")
-    yield
-    for copy in copies:
-        copy.wait()
-    for f in range(n):
-        for i in range(cx):
-            x = turned[f, i]
-            plus = jnp.concatenate([x[1:], ybox[0, f, i : i + 1, :]], axis=0)
-            minus = jnp.concatenate([ybox[1, f, i : i + 1, :], x[: cy - 1]], axis=0)
-            put(f, i, jnp.where(ups[f][1], plus, minus))
+            plus = core[i + 1] if i + 1 < cx else side
+            minus = core[i - 1] if i > 0 else side
+            x = jnp.where(up_x, plus, minus)
+            plus = face[i + 1 : i + 2] if i + 1 < cx else corner
+            minus = face[i - 1 : i] if i > 0 else corner
+            row = jnp.where(up_x, plus, minus)
+            plus = jnp.concatenate([x[1:], row], axis=0)
+            minus = jnp.concatenate([row, x[: cy - 1]], axis=0)
+            put(f, i, jnp.where(up_y, plus, minus))
 
 
 def shift_scratch(shape, kind):
     n, cx, cy, nz = shape
     return [
-        pltpu.VMEM((2, n, cx, cy, nz), kind), pltpu.VMEM((2, n, cy, nz), kind),
-        pltpu.VMEM((2, n, cx, nz), kind), pltpu.VMEM((n, cx, cy, nz), kind),
-        pltpu.VMEM((n, cx, cy, nz), kind), pltpu.VMEM((2, n, cx, nz), kind),
+        pltpu.VMEM((2, n, cx, cy, nz), kind), pltpu.VMEM((2, 3, n, cy, nz), kind),
+        pltpu.VMEM((3, 2, 3, n, cx, nz), kind), pltpu.VMEM((2, n, cx, nz), kind),
     ]
-
-
-def beside_work(transfer, step, count):
-    for part in range(4):
-        next(transfer)
-        lax.fori_loop(count * part // 4, count * (part + 1) // 4, step, 0)
-    for _ in transfer:
-        pass
 
 
 def contact_places(colloid, units):
@@ -272,12 +295,12 @@
 
 
 def main_kernel(
-    per, units, shift_ref, v_in, cs, axis_hbm, dir_hbm, slot_hbm, who_hbm, colloid_hbm, weight_hbm, drift_ref,
+    per, units, shift_hbm, v_in, cs, axis_hbm, dir_hbm, slot_hbm, who_hbm, colloid_hbm, weight_hbm, drift_hbm,
     kept_ref, tail_ref, cellv_ref, force_ref,
-    vs, field, dirs, slots, who, colloid, weight, axes, mean, field_mean, table, unit_ref, st, acc, moved, book,
+    vs, shift_ref, drift_ref, field, dirs, slots, who, colloid, weight, axes, mean, field_mean, table, unit_ref, st, acc, moved, book,
     going, coming, pushes, pulls, *rest
 ):
-    boxes_a, boxes_b, (local_sem, out_sem, in_sem) = rest[:6], rest[6:12], rest[12:]
+    boxes_a, boxes_b, (local_sem, out_sem, in_sem) = rest[:4], rest[4:8], rest[8:]
     sems = (out_sem, in_sem)
     cx, cy, nz = axis_hbm.shape[1:]
     groups = v_in.shape[1]
@@ -288,19 +311,15 @@
         copy.start()
         return copy
 
-    first = [fetch(axis_hbm, field, 0)]
+    first = [fetch(axis_hbm, field, 0), fetch(shift_hbm, shift_ref, 7)]
     late = [fetch(dir_hbm, dirs, 1), fetch(slot_hbm, slots, 2), fetch(who_hbm, who, 3)]
-    late += [fetch(colloid_hbm, colloid, 4), fetch(weight_hbm, weight, 5)]
+    late += [fetch(colloid_hbm, colloid, 4), fetch(weight_hbm, weight, 5), fetch(drift_hbm, drift_ref, 6)]
     greet()
 
     steps = iotas(LO)
 
     def rows_of(t, u):
         return pl.ds(pl.multiple_of((t * per + u) * 8, 8), 8)
-
-    def meet():
-        pl.semaphore_wait(pltpu.get_barrier_semaphore(), 6)
-        first[0].wait()
 
     def put_axis(f, i, value):
         axes[f, i * cy : (i + 1) * cy, :] = value
@@ -314,8 +333,13 @@
         hist_add(acc, st, range(per), steps)
         return carry
 
-    transfer = shift_fields((0, 1), 1, shift_ref, field, put_axis, boxes_a, sems, 0, meet)
-    beside_work(transfer, step0, loops)
+    lax.fori_loop(0, EARLY, step0, 0)
+    pl.semaphore_wait(pltpu.get_barrier_semaphore(), len(kept_ways()))
+    for copy in first:
+        copy.wait()
+    copies = start_shift(field, boxes_a, sems, 0)
+    lax.fori_loop(EARLY, loops, step0, 0)
+    finish_shift(copies, (0, 1), 1, shift_ref, field, boxes_a, put_axis)
     mean_of(acc[...], mean)
     for copy in late:
         copy.wait()
@@ -385,10 +409,8 @@
         cellv_ref[f, i] = value
 
     rows_of_shift = [shift_ref.shape[0] - 1] * 3
-    transfer = shift_fields(
-        rows_of_shift, -1, shift_ref, field_mean, put_mean, boxes_b, sems, 6, lambda: None
-    )
-    beside_work(transfer, step2, loops)
+    means = start_shift(field_mean, boxes_b, sems, 26)
+    lax.fori_loop(0, loops, step2, 0)
 
     for k in range(3):
         value = moved[32 * k : 32 * k + 16] + moved[32 * k + 16 : 32 * k + 32]
@@ -401,7 +423,7 @@
                 at += size
             going[d, k : k + 1, :] = jnp.concatenate(parts, axis=1)
     copies = [
-        send(going.at[d], coming.at[d], sems, 12 + d, AXES[d // 2], 1 - 2 * (d % 2)) for d in range(6)
+        send(going.at[d], coming.at[d], sems, 52 + d, AXES[d // 2], 1 - 2 * (d % 2)) for d in range(6)
     ]
 
     contacts = who.shape[1]
@@ -430,8 +452,9 @@
         for k in range(4):
             pushes[d, k : k + 1, :] = totals[k][d : d + 1]
     more = [
-        send(pushes.at[d], pulls.at[d], sems, 18 + d, AXES[d // 2], 1 - 2 * (d % 2)) for d in range(6)
+        send(pushes.at[d], pulls.at[d], sems, 58 + d, AXES[d // 2], 1 - 2 * (d % 2)) for d in range(6)
     ]
+    finish_shift(means, rows_of_shift, -1, shift_ref, field_mean, boxes_b, put_mean)
     for d, copy in enumerate(copies):
         copy.wait()
         for k in range(3):
@@ -470,10 +493,9 @@
     cells = (cx * cy, nlo)
     if cells != (2 * HI, 128) or particles % 4096 or 6 * CAP > 16 * SLOT:
         raise ValueError("sizes")
-    per = 4
+    per = next(p for p in (8, 4) if groups % (8 * p) == 0)
     grid_mean = (3, cx, cy, nlo)
     vmem = pl.BlockSpec(memory_space=pltpu.VMEM)
-    smem = pl.BlockSpec(memory_space=pltpu.SMEM)
     hbm = pl.BlockSpec(memory_space=pl.ANY)
     outs = (
         jax.ShapeDtypeStruct((3, groups, 128), F32),
@@ -482,13 +504,18 @@
         jax.ShapeDtypeStruct((3, units), F32),
     )
     dma = pltpu.SemaphoreType.DMA
+
+    def stay(x):
+        return pltpu.with_memory_space_constraint(x, pltpu.HBM)
+
     kept, tail, cellv, force = pl.pallas_call(
         functools.partial(main_kernel, per, units),
         out_shape=outs,
-        in_specs=[smem] + [vmem] * 2 + [hbm] * 6 + [vmem],
+        in_specs=[hbm] + [vmem] * 2 + [hbm] * 7,
         out_specs=(vmem,) * 4,
         scratch_shapes=[
-            pltpu.VMEM((3, groups, 128), F32), pltpu.VMEM(axis_index.shape, I32), pltpu.VMEM((groups, 128), I32), pltpu.VMEM((groups, 128), I32),
+            pltpu.VMEM((3, groups, 128), F32), pltpu.SMEM(grid_shift.shape, I32), pltpu.VMEM((3, units), F32),
+            pltpu.VMEM(axis_index.shape, I32), pltpu.VMEM((groups, 128), I32), pltpu.VMEM((groups, 128), I32),
             pltpu.VMEM((1, contacts), I32), pltpu.VMEM((1, contacts), I32), pltpu.VMEM((1, contacts), F32),
             pltpu.VMEM((2,) + cells, I32), pltpu.VMEM((3,) + cells, F32), pltpu.VMEM(grid_mean, F32),
             pltpu.VMEM((2,) + cells, I32), pltpu.VMEM((8, 128), F32), pltpu.VMEM((per, PLANES + 1, 8, 128), F32),
@@ -497,15 +524,15 @@
             pltpu.VMEM((6, 4, units), F32), pltpu.VMEM((6, 4, units), F32),
         ]
         + shift_scratch(axis_index.shape, I32) + shift_scratch(grid_mean, F32)
-        + [dma((6,)), dma((24,)), dma((24,))],
+        + [dma((8,)), dma((64,)), dma((64,))],
         compiler_params=pltpu.CompilerParams(
             vmem_limit_bytes=48 * 2**20, collective_id=0, has_side_effects=True
         ),
         cost_estimate=pl.CostEstimate(flops=10**9, bytes_accessed=30_000_000, transcendentals=0),
     )(
-        grid_shift, velocities.reshape(3, groups, 128), particle_cells.reshape(2, groups, 128), axis_index, migrate_dir.reshape(groups, 128),
-        migrate_slot.reshape(groups, 128), contact_particle.reshape(1, -1), contact_colloid.reshape(1, -1),
-        contact_weight.reshape(1, -1), colloid_velocity,
+        stay(grid_shift), velocities.reshape(3, groups, 128), particle_cells.reshape(2, groups, 128), stay(axis_index), stay(migrate_dir.reshape(groups, 128)),
+        stay(migrate_slot.reshape(groups, 128)), stay(contact_particle.reshape(1, -1)),
+        stay(contact_colloid.reshape(1, -1)), stay(contact_weight.reshape(1, -1)), stay(colloid_velocity),
     )
     return pl.pallas_call(
         last_kernel,

time: 42 us -> 32.1 us (0.76)
  Pallas kernels: 39 us -> 30.1 us
  local copies, waits for them, and re-layouts: 2.14 us -> 1.21 us
    pallas_call x1, Pallas kernels: 38.2 us -> 29.2 us  [body(): pl.pallas_call(functools.partial(main_kernel, per, units), out_shape=outs...]
    unnamed x20 -> x4, local copies, waits for them, and re-layouts: 2.14 us -> 1.21 us
where the time goes in v2:
time: 32.1 us; the launch traced here: 31.9 us
  Pallas kernels  30.1 us (94%)
  local copies, waits for them, and re-layouts  1.21 us (4%)
  between operations  0.65 us (2%)
    pallas_call x1, Pallas kernels, body(): pl.pallas_call(functools.partial(main_kernel, per, units), out_shape=outs...  29.2 us
    unnamed x4, local copies, waits for them, and re-layouts  1.21 us
    pallas_call x1, Pallas kernels, body(): pl.pallas_call(last_kernel, out_shape=(jax.ShapeDtypeStruct(grid_mean, F3...  0.87 us

profile of v2, /device:TPU:0, one launch (start us, length us, event | category | flops | bytes accessed | tf_op | source)
XLA Modules:
  0.0 31.9 jit_solution(17067110084607690693)
XLA Ops:
  0.6 0.0 copy-start
  0.6 1.1 %copy.18 = s32[1,2,320,128]{3,2,1,0:T(8,128)S(1)} copy(s32[1,2,320,128]{3,1,2,0:T(2,128)} %bitcast.18) | data formatting | bytes 655360
  1.7 0.1 copy-done
  1.9 29.2 %shard_map.121 = (f32[3,320,128]{2,1,0:T(8,128)S(1)}, f32[3,1,960]{2,1,0:T(1,128)S(1)}, f32[3,4,8,128]{3,2,1,0:T(8,128)S(1)}, f32[3,256]{1,0:T(4,128)S(1)}) custom-call(s32[2,3]{1,0:T(2,128)} %shift_hbm.1, f32[3,320,128]{2,1,0:T(8,128)S(1)} %bitcast.15, s32[2,320,128]{2,1,0:T(8,128)S(1)} %bitcast.16, s32[2,4,8,128]{3,2,1,0:T(8,128)} %axis_hbm.1, ...), custom_call_target="tpu_custom_call" | custom-call | flops 1000000000 | bytes 30000000 | tf_op jit(solution)/shard_map/pallas_call | solution.py:511
  31.1 0.9 %shard_map.122 = (f32[3,4,8,128]{3,2,1,0:T(8,128)}, f32[3,41920]{1,0:T(4,128)}, f32[3,256]{1,0:T(4,128)}) custom-call(f32[3,1,40960]{2,1,0:T(1,128)S(1)} %bitcast.14, f32[3,1,960]{2,1,0:T(1,128)S(1)} %get-tuple-element.8.tail_ref, f32[3,4,8,128]{3,2,1,0:T(8,128)S(1)} %get-tuple-element.9.cellv_ref, f32[3,256]{1,0:T(4,128)S(1)} %get-tuple-element.10.force_ref), custom_call_target="tpu_custom_call" | custom-call | tf_op jit(solution)/shard_map/pallas_call | solution.py:537
  (1 shorter events, 0.0 us)
Async XLA Ops:
  0.6 1.2 %copy-start = (f32[3,40960]{1,0:T(4,128)S(1)}, f32[3,40960]{1,0:T(4,128)}, u32[]{:S(2)}) copy-start(f32[3,40960]{1,0:T(4,128)} %param.10) | copy-start | bytes 1474564

commit v3 on v2

--- a/solution.py
+++ b/solution.py
@@ -304,7 +304,7 @@
     sems = (out_sem, in_sem)
     cx, cy, nz = axis_hbm.shape[1:]
     groups = v_in.shape[1]
-    loops = groups // (8 * per)
+    loops0, loops = groups // (8 * per[0]), groups // (8 * per[1])
 
     def fetch(src, dst, number):
         copy = pltpu.make_async_copy(src, dst, local_sem.at[number])
@@ -318,8 +318,8 @@
 
     steps = iotas(LO)
 
-    def rows_of(t, u):
-        return pl.ds(pl.multiple_of((t * per + u) * 8, 8), 8)
+    def rows_of(t, u, many):
+        return pl.ds(pl.multiple_of((t * many + u) * 8, 8), 8)
 
     def put_axis(f, i, value):
         axes[f, i * cy : (i + 1) * cy, :] = value
@@ -327,10 +327,10 @@
     acc[...] = jnp.zeros_like(acc)
 
     def step0(t, carry):
-        for u in range(per):
-            at = rows_of(t, u)
+        for u in range(per[0]):
+            at = rows_of(t, u, per[0])
             stage_hist(st.at[u], cs[0, at], [v_in[k, at] for k in range(3)])
-        hist_add(acc, st, range(per), steps)
+        hist_add(acc, st, range(per[0]), steps)
         return carry
 
     lax.fori_loop(0, EARLY, step0, 0)
@@ -338,7 +338,7 @@
     for copy in first:
         copy.wait()
     copies = start_shift(field, boxes_a, sems, 0)
-    lax.fori_loop(EARLY, loops, step0, 0)
+    lax.fori_loop(EARLY, loops0, step0, 0)
     finish_shift(copies, (0, 1), 1, shift_ref, field, boxes_a, put_axis)
     mean_of(acc[...], mean)
     for copy in late:
@@ -348,13 +348,13 @@
 
     def step1(t, carry):
         unit = unit_ref[...]
-        for u in range(per):
-            at = rows_of(t, u)
+        for u in range(per[1]):
+            at = rows_of(t, u, per[1])
             new = collide(table, unit, cs[0, at], [v_in[k, at] for k in range(3)])
             for k in range(3):
                 vs[k, at] = new[k]
             stage_hist(st.at[u], cs[1, at], new)
-        hist_add(acc, st, range(per), steps)
+        hist_add(acc, st, range(per[1]), steps)
         return carry
 
     lax.fori_loop(0, loops, step1, 0)
@@ -376,8 +376,8 @@
     def step2(t, carry):
         unit = unit_ref[...]
         hots, lefts = [], []
-        for u in range(per):
-            at = rows_of(t, u)
+        for u in range(per[1]):
+            at = rows_of(t, u, per[1])
             new = collide(table, unit, cs[1, at], [vs[k, at] for k in range(3)])
             code = dirs[at]
             stays = code == 0
@@ -389,13 +389,13 @@
                 high, low = halves(new[k])
                 st[u, 2 + 2 * k] = high.astype(F32)
                 st[u, 3 + 2 * k] = low.astype(F32)
-        for u in range(0, per, 2):
-            at = pl.ds(pl.multiple_of((t * per + u) * 8, 16), 16)
+        for u in range(0, per[1], 2):
+            at = pl.ds(pl.multiple_of((t * per[1] + u) * 8, 16), 16)
             for k in range(3):
                 for i in range(2):
                     both_tiles = jnp.concatenate([st[u, 2 + 2 * k + i], st[u + 1, 2 + 2 * k + i]], axis=0)
                     book[k, at, i * 128 : (i + 1) * 128] = both_tiles.astype(BF)
-        for u in range(per):
+        for u in range(per[1]):
             for j in range(8):
                 hot, left = leave_group(st.at[u], j)
                 hots.append(hot)
@@ -493,7 +493,7 @@
     cells = (cx * cy, nlo)
     if cells != (2 * HI, 128) or particles % 4096 or 6 * CAP > 16 * SLOT:
         raise ValueError("sizes")
-    per = next(p for p in (8, 4) if groups % (8 * p) == 0)
+    per = [next(p for p in sizes if groups % (8 * p) == 0) for sizes in ((8, 4), (20, 8, 4))]
     grid_mean = (3, cx, cy, nlo)
     vmem = pl.BlockSpec(memory_space=pltpu.VMEM)
     hbm = pl.BlockSpec(memory_space=pl.ANY)
@@ -518,7 +518,7 @@
             pltpu.VMEM(axis_index.shape, I32), pltpu.VMEM((groups, 128), I32), pltpu.VMEM((groups, 128), I32),
             pltpu.VMEM((1, contacts), I32), pltpu.VMEM((1, contacts), I32), pltpu.VMEM((1, contacts), F32),
             pltpu.VMEM((2,) + cells, I32), pltpu.VMEM((3,) + cells, F32), pltpu.VMEM(grid_mean, F32),
-            pltpu.VMEM((2,) + cells, I32), pltpu.VMEM((8, 128), F32), pltpu.VMEM((per, PLANES + 1, 8, 128), F32),
+            pltpu.VMEM((2,) + cells, I32), pltpu.VMEM((8, 128), F32), pltpu.VMEM((max(per), PLANES + 1, 8, 128), F32),
             pltpu.VMEM((PLANES * HI, LO), F32), pltpu.VMEM((96, SLOT), F32), pltpu.VMEM((3, groups, 256), BF),
             pltpu.VMEM((6, 3, CAP), F32), pltpu.VMEM((6, 3, CAP), F32),
             pltpu.VMEM((6, 4, units), F32), pltpu.VMEM((6, 4, units), F32),

time: 32.1 us -> 30.8 us (0.960)
  Pallas kernels: 30.1 us -> 28.8 us
    pallas_call x1, Pallas kernels: 29.2 us -> 28 us  [body(): pl.pallas_call(functools.partial(main_kernel, per, units), out_shape=outs...]
where the time goes in v3:
time: 30.8 us; the launch traced here: 30.7 us
  Pallas kernels  28.8 us (94%)
  local copies, waits for them, and re-layouts  1.21 us (4%)
  between operations  0.65 us (2%)
    pallas_call x1, Pallas kernels, body(): pl.pallas_call(functools.partial(main_kernel, per, units), out_shape=outs...  28 us
    unnamed x4, local copies, waits for them, and re-layouts  1.21 us
    pallas_call x1, Pallas kernels, body(): pl.pallas_call(last_kernel, out_shape=(jax.ShapeDtypeStruct(grid_mean, F3...  0.87 us

profile of v3, /device:TPU:0, one launch (start us, length us, event | category | flops | bytes accessed | tf_op | source)
XLA Modules:
  0.0 30.7 jit_solution(7756767681563511632)
XLA Ops:
  0.6 0.0 copy-start
  0.6 1.1 %copy.18 = s32[1,2,320,128]{3,2,1,0:T(8,128)S(1)} copy(s32[1,2,320,128]{3,1,2,0:T(2,128)} %bitcast.18) | data formatting | bytes 655360
  1.7 0.1 copy-done
  1.9 28.0 %shard_map.121 = (f32[3,320,128]{2,1,0:T(8,128)S(1)}, f32[3,1,960]{2,1,0:T(1,128)S(1)}, f32[3,4,8,128]{3,2,1,0:T(8,128)S(1)}, f32[3,256]{1,0:T(4,128)S(1)}) custom-call(s32[2,3]{1,0:T(2,128)} %shift_hbm.1, f32[3,320,128]{2,1,0:T(8,128)S(1)} %bitcast.15, s32[2,320,128]{2,1,0:T(8,128)S(1)} %bitcast.16, s32[2,4,8,128]{3,2,1,0:T(8,128)} %axis_hbm.1, ...), custom_call_target="tpu_custom_call" | custom-call | flops 1000000000 | bytes 30000000 | tf_op jit(solution)/shard_map/pallas_call | solution.py:511
  29.8 0.9 %shard_map.122 = (f32[3,4,8,128]{3,2,1,0:T(8,128)}, f32[3,41920]{1,0:T(4,128)}, f32[3,256]{1,0:T(4,128)}) custom-call(f32[3,1,40960]{2,1,0:T(1,128)S(1)} %bitcast.14, f32[3,1,960]{2,1,0:T(1,128)S(1)} %get-tuple-element.8.tail_ref, f32[3,4,8,128]{3,2,1,0:T(8,128)S(1)} %get-tuple-element.9.cellv_ref, f32[3,256]{1,0:T(4,128)S(1)} %get-tuple-element.10.force_ref), custom_call_target="tpu_custom_call" | custom-call | tf_op jit(solution)/shard_map/pallas_call | solution.py:537
  (1 shorter events, 0.0 us)
Async XLA Ops:
  0.6 1.2 %copy-start = (f32[3,40960]{1,0:T(4,128)S(1)}, f32[3,40960]{1,0:T(4,128)}, u32[]{:S(2)}) copy-start(f32[3,40960]{1,0:T(4,128)} %param.10) | copy-start | bytes 1474564

commit v4 on v3

--- a/solution.py
+++ b/solution.py
@@ -25,6 +25,7 @@
 AXES = ("gx", "gy", "gz")
 MESH = pl.DeviceIdType.MESH
 WAYS = [(x, y, z) for x in (-1, 0, 1) for y in (-1, 0, 1) for z in (-1, 0, 1) if (x, y, z) != (0, 0, 0)]
+WAYS.sort(key=lambda way: (way[0] == 0, -sum(map(abs, way))))
 
 
 def split_index(c, low):

time: 30.8 us -> 30.8 us (level)
  no operation moved by 1% of the time
where the time goes in v4:
time: 30.8 us; the launch traced here: 30.7 us
  Pallas kernels  28.8 us (94%)
  local copies, waits for them, and re-layouts  1.21 us (4%)
  between operations  0.65 us (2%)
    pallas_call x1, Pallas kernels, body(): pl.pallas_call(functools.partial(main_kernel, per, units), out_shape=outs...  28 us
    unnamed x4, local copies, waits for them, and re-layouts  1.21 us
    pallas_call x1, Pallas kernels, body(): pl.pallas_call(last_kernel, out_shape=(jax.ShapeDtypeStruct(grid_mean, F3...  0.87 us

profile of v4, /device:TPU:0, one launch (start us, length us, event | category | flops | bytes accessed | tf_op | source)
XLA Modules:
  0.0 30.7 jit_solution(10776896923678773553)
XLA Ops:
  0.6 0.0 copy-start
  0.6 1.1 %copy.18 = s32[1,2,320,128]{3,2,1,0:T(8,128)S(1)} copy(s32[1,2,320,128]{3,1,2,0:T(2,128)} %bitcast.18) | data formatting | bytes 655360
  1.7 0.1 copy-done
  1.9 28.0 %shard_map.121 = (f32[3,320,128]{2,1,0:T(8,128)S(1)}, f32[3,1,960]{2,1,0:T(1,128)S(1)}, f32[3,4,8,128]{3,2,1,0:T(8,128)S(1)}, f32[3,256]{1,0:T(4,128)S(1)}) custom-call(s32[2,3]{1,0:T(2,128)} %shift_hbm.1, f32[3,320,128]{2,1,0:T(8,128)S(1)} %bitcast.15, s32[2,320,128]{2,1,0:T(8,128)S(1)} %bitcast.16, s32[2,4,8,128]{3,2,1,0:T(8,128)} %axis_hbm.1, ...), custom_call_target="tpu_custom_call" | custom-call | flops 1000000000 | bytes 30000000 | tf_op jit(solution)/shard_map/pallas_call | solution.py:512
  29.8 0.9 %shard_map.122 = (f32[3,4,8,128]{3,2,1,0:T(8,128)}, f32[3,41920]{1,0:T(4,128)}, f32[3,256]{1,0:T(4,128)}) custom-call(f32[3,1,40960]{2,1,0:T(1,128)S(1)} %bitcast.14, f32[3,1,960]{2,1,0:T(1,128)S(1)} %get-tuple-element.8.tail_ref, f32[3,4,8,128]{3,2,1,0:T(8,128)S(1)} %get-tuple-element.9.cellv_ref, f32[3,256]{1,0:T(4,128)S(1)} %get-tuple-element.10.force_ref), custom_call_target="tpu_custom_call" | custom-call | tf_op jit(solution)/shard_map/pallas_call | solution.py:538
  (1 shorter events, 0.0 us)
Async XLA Ops:
  0.6 1.2 %copy-start = (f32[3,40960]{1,0:T(4,128)S(1)}, f32[3,40960]{1,0:T(4,128)}, u32[]{:S(2)}) copy-start(f32[3,40960]{1,0:T(4,128)} %param.10) | copy-start | bytes 1474564
